TPU v7x, 32 devices: a whole 2x2x4 slice. The times are simulated.
32 devices in a mesh: aa: 4 (over x, core), ba: 8 (over z, y).
Axes of the slice: x: 2, y: 2, z: 4, core: 2. Of those that a mesh axis runs over, the one named last changes fastest.
Arguments:
- initial_dictionary_matrix: bfloat16 [32768, 3584], P('ba', 'aa'), may hold values from -60 to 60
- decoder_two: bfloat16 [32768, 3584], P('ba', 'aa'), may hold values from -60 to 60
- route_one: int32 [8, 8], replicated, may hold values from 0 to 7
- route_two: int32 [8, 8], replicated, may hold values from 0 to 7
- candidate_pair_slots: int32 [8, 24, 2], P('ba'), may hold values from 0 to 7
Outputs:
- leading_logarithmic_factor: float32 [32768], P('ba')
- col_log_scale: float32 [32768], P('ba')
All inputs are finite; a program needn't handle non-finite values.
Results may differ from a plain program's by a relative error of at most 0.00046.
Values may be sent and summed in bfloat16 or wider, within the bound.
A program may use at most 128 MiB of HBM per device.

v0:
```python
import jax
import jax.numpy as jnp
from jax import lax
from jax.sharding import PartitionSpec as P

BS = 512
SWEEPS = 4


smoothing_regularizer = 0.02
norm_floor = 1e-06


def converge_balancing(partial_totals):
    totals = lax.psum(partial_totals, ("aa", "ba"))
    return 1.0 / (1.0 + totals)


def per_device(initial_dictionary_matrix, decoder_two, route_one, route_two, candidate_pair_slots):
    column = lax.axis_index("ba")
    depth = lax.axis_size("aa")
    depth_index = lax.axis_index("aa")
    owners = lax.axis_size("ba")
    width = initial_dictionary_matrix.shape[1]
    blocks_dev = initial_dictionary_matrix.shape[0] // BS
    nblocks = blocks_dev * owners
    sum_one = jnp.sum(jnp.square(initial_dictionary_matrix.astype(jnp.float32)), axis=1)
    sum_two = jnp.sum(jnp.square(decoder_two.astype(jnp.float32)), axis=1)
    sum_one, sum_two = lax.psum((sum_one, sum_two), "aa")
    unit_one = (
        initial_dictionary_matrix.astype(jnp.float32) * lax.rsqrt(sum_one + norm_floor)[:, None]
    ).astype(jnp.bfloat16)
    unit_two = (decoder_two.astype(jnp.float32) * lax.rsqrt(sum_two + norm_floor)[:, None]).astype(
        jnp.bfloat16
    )
    send_one = jnp.take(unit_one.reshape(blocks_dev, BS, width), route_one[column], axis=0)
    second_seed_sender = jnp.take(
        unit_two.reshape(blocks_dev, BS, width), route_two[column], axis=0
    )
    got_one, got_two = (
        lax.all_to_all(send_one, "ba", split_axis=0, concat_axis=0, tiled=True),
        lax.all_to_all(second_seed_sender, "ba", split_axis=0, concat_axis=0, tiled=True),
    )
    column_pairs = candidate_pair_slots[0]
    whole_pairs = column_pairs.shape[0]
    owned = whole_pairs // depth
    left = jnp.take(got_one, column_pairs[:, 0], axis=0)
    right = jnp.take(got_two, column_pairs[:, 1], axis=0)
    angular_agreement = lax.psum_scatter(
        jnp.einsum("qid,qjd->qij", left, right, preferred_element_type=jnp.float32),
        "aa",
        scatter_dimension=0,
        tiled=True,
    )
    exponential_affinity = jnp.exp(angular_agreement / smoothing_regularizer)
    my_pairs = lax.dynamic_slice_in_dim(column_pairs, depth_index * owned, owned, 0)
    row_ids = my_pairs[:, 0] * blocks_dev + route_one[:, column][my_pairs[:, 0]]
    col_ids = my_pairs[:, 1] * blocks_dev + route_two[:, column][my_pairs[:, 1]]
    block_ids = jnp.arange(nblocks, dtype=jnp.int32)
    row_hot = (row_ids[:, None] == block_ids[None, :]).astype(jnp.float32)
    col_hot = (col_ids[:, None] == block_ids[None, :]).astype(jnp.float32)
    col_scale = jnp.ones((nblocks, BS), jnp.float32)
    row_scale = jnp.ones((nblocks, BS), jnp.float32)
    for sweep_index in range(SWEEPS):
        row_terms = jnp.einsum(
            "qij,qj->qi",
            exponential_affinity,
            jnp.take(col_scale, col_ids, axis=0),
            precision=lax.Precision.HIGHEST,
        )
        row_scale = converge_balancing(
            jnp.einsum("qb,qi->bi", row_hot, row_terms, precision=lax.Precision.HIGHEST)
        )
        col_terms = jnp.einsum(
            "qij,qi->qj",
            exponential_affinity,
            jnp.take(row_scale, row_ids, axis=0),
            precision=lax.Precision.HIGHEST,
        )
        col_scale = converge_balancing(
            jnp.einsum("qb,qj->bj", col_hot, col_terms, precision=lax.Precision.HIGHEST)
        )
    row_mine = lax.dynamic_slice_in_dim(row_scale, column * blocks_dev, blocks_dev, 0)
    column_local_part = lax.dynamic_slice_in_dim(col_scale, column * blocks_dev, blocks_dev, 0)
    return (jnp.log(row_mine).reshape(-1), jnp.log(column_local_part).reshape(-1))


def solution(mesh):
    placed = (P("ba", "aa"), P("ba", "aa"), P(), P(), P("ba", None, None))
    return jax.shard_map(
        per_device, mesh=mesh, in_specs=placed, out_specs=(P("ba"), P("ba")), check_vma=False
    )
```

profile of v0, /device:TPU:0, one launch (start us, length us, event | category | flops | bytes accessed | tf_op | source)
XLA Modules:
  0.0 1678.7 jit_solution(7892259898923653426)
XLA Ops:
  13.8 12.9 all-reduce
  26.8 7.3 fusion.8
  34.2 7.5 gather_fusion.4
  41.7 6.9 broadcast_select_fusion
  54.4 7.3 fusion.6
  61.7 7.4 gather_fusion.2
  76.0 138.1 %all-to-all-done.1 = bf16[8,512,896]{2,1,0:T(8,128)(2,1)} async-done(((bf16[8,512,896]{2,1,0:T(8,128)(2,1)}), bf16[8,512,896]{2,1,0:T(8,128)(2,1)}, u32[]{:S(2)}, u32[]{:S(2)}) %all-to-all-start.1) | async-done | bytes 7340064 | tf_op jit(solution)/shard_map/all_to_all | solution.py:42
  219.6 12.8 gather_fusion.5
  232.4 146.2 %all-to-all-done = bf16[8,512,896]{2,1,0:T(8,128)(2,1)} async-done(((bf16[8,512,896]{2,1,0:T(8,128)(2,1)}), bf16[8,512,896]{2,1,0:T(8,128)(2,1)}, u32[]{:S(2)}, u32[]{:S(2)}) %all-to-all-start) | async-done | bytes 7340064 | tf_op jit(solution)/shard_map/all_to_all | solution.py:41
  378.6 12.6 gather_fusion.3
  391.3 26.2 %fusion = f32[24,512,512]{2,1,0:T(8,128)} fusion(bf16[24,512,896]{2,1,0:T(8,128)(2,1)} %gather_fusion.5, bf16[24,512,896]{2,1,0:T(8,128)(2,1)} %gather_fusion.3, pred[24]{0:T(512)(128)(4,1)S(1)} %get-tuple-element.23, pred[24]{0:T(512)(128)(4,1)S(1)} %get-tuple-element.11), kind=kOutput, calls=%fused_computation.14 | convolution fusion | flops 11296309248 | bytes 69206064 | tf_op jit(solution)/shard_map/qid,qjd->qij/dot_general | solution.py:50
  420.0 179.3 %reduce-scatter.2.cloned.1.call-done = f32[6,512,512]{2,1,0:T(8,128)} async-done(((f32[24,512,512]{2,1,0:T(8,128)}), f32[6,512,512]{2,1,0:T(8,128)}) %reduce-scatter.2.cloned.1.call-update) | async-done | bytes 6291472 | tf_op jit(solution)/shard_map/reduce_scatter | solution.py:49
  599.3 8.7 fusion.17
  609.2 124.4 %all-reduce.10.cloned.1.call-done = f32[64,512]{1,0:T(8,128)} async-done(((f32[64,512]{1,0:T(8,128)}), f32[64,512]{1,0:T(8,128)}) %all-reduce.10.cloned.1.call-update) | async-done | bytes 131088 | tf_op jit(solution)/shard_map/psum | solution.py:15
  742.9 123.6 %all-reduce.12.cloned.1.call-done = f32[64,512]{1,0:T(8,128)} async-done(((f32[64,512]{1,0:T(8,128)}), f32[64,512]{1,0:T(8,128)}) %all-reduce.12.cloned.1.call-update) | async-done | bytes 131088 | tf_op jit(solution)/shard_map/psum | solution.py:15
  868.1 8.7 fusion.15
  878.1 123.4 %all-reduce.14.cloned.1.call-done = f32[64,512]{1,0:T(8,128)} async-done(((f32[64,512]{1,0:T(8,128)}), f32[64,512]{1,0:T(8,128)}) %all-reduce.14.cloned.1.call-update) | async-done | bytes 131088 | tf_op jit(solution)/shard_map/psum | solution.py:15
  1010.9 123.6 %all-reduce.16.cloned.1.call-done = f32[64,512]{1,0:T(8,128)} async-done(((f32[64,512]{1,0:T(8,128)}), f32[64,512]{1,0:T(8,128)}) %all-reduce.16.cloned.1.call-update) | async-done | bytes 131088 | tf_op jit(solution)/shard_map/psum | solution.py:15
  1136.1 8.7 fusion.13
  1146.1 123.4 %all-reduce.18.cloned.1.call-done = f32[64,512]{1,0:T(8,128)} async-done(((f32[64,512]{1,0:T(8,128)}), f32[64,512]{1,0:T(8,128)}) %all-reduce.18.cloned.1.call-update) | async-done | bytes 131088 | tf_op jit(solution)/shard_map/psum | solution.py:15
  1278.8 123.6 %all-reduce.20.cloned.1.call-done = f32[64,512]{1,0:T(8,128)} async-done(((f32[64,512]{1,0:T(8,128)}), f32[64,512]{1,0:T(8,128)}) %all-reduce.20.cloned.1.call-update) | async-done | bytes 131088 | tf_op jit(solution)/shard_map/psum | solution.py:15
  1404.0 8.7 fusion.11
  1414.0 123.3 %all-reduce.22.cloned.1.call-done = f32[64,512]{1,0:T(8,128)} async-done(((f32[64,512]{1,0:T(8,128)}), f32[64,512]{1,0:T(8,128)}) %all-reduce.22.cloned.1.call-update) | async-done | bytes 131088 | tf_op jit(solution)/shard_map/psum | solution.py:15
  1547.3 123.0 %all-reduce.24.cloned.1.call-done = f32[64,512]{1,0:T(8,128)} async-done(((f32[64,512]{1,0:T(8,128)}), f32[64,512]{1,0:T(8,128)}) %all-reduce.24.cloned.1.call-update) | async-done | bytes 131088 | tf_op jit(solution)/shard_map/psum | solution.py:15
  (90 shorter events, 76.2 us)
Async XLA Ops:
  7.2 5.2 copy-start
  26.8 7.4 copy-start.1
  26.8 7.4 copy-start.2
  48.6 165.6 %all-to-all-start.1 = ((bf16[8,512,896]{2,1,0:T(8,128)(2,1)}), bf16[8,512,896]{2,1,0:T(8,128)(2,1)}, u32[]{:S(2)}, u32[]{:S(2)}) async-start(bf16[8,512,896]{2,1,0:T(8,128)(2,1)} %broadcast_select_fusion), calls=%async_computation.1 | async-start | bytes 14680064 | tf_op jit(solution)/shard_map/all_to_all | solution.py:42
  76.0 143.6 %copy-start.3 = (s32[1,24,2]{1,2,0:T(2,128)S(1)}, s32[1,24,2]{1,2,0:T(2,128)}, u32[]{:S(2)}) copy-start(s32[1,24,2]{1,2,0:T(2,128)} %param.15) | copy-start | bytes 580
  214.1 164.5 %all-to-all-start = ((bf16[8,512,896]{2,1,0:T(8,128)(2,1)}), bf16[8,512,896]{2,1,0:T(8,128)(2,1)}, u32[]{:S(2)}, u32[]{:S(2)}) async-start(bf16[8,512,896]{2,1,0:T(8,128)(2,1)} %broadcast_select_fusion.1), calls=%async_computation | async-start | bytes 14680064 | tf_op jit(solution)/shard_map/all_to_all | solution.py:41
  219.0 380.3 %reduce-scatter.2.cloned.1.call-start = ((), (), s32[]{:S(2)}) async-start(), calls=%async_computation.3 | async-start | bytes 31457280 | tf_op jit(solution)/shard_map/reduce_scatter | solution.py:49
  417.5 316.2 %all-reduce.10.cloned.1.call-start = ((), (), s32[]{:S(2)}) async-start(), calls=%async_computation.4 | async-start | bytes 262144 | tf_op jit(solution)/shard_map/psum | solution.py:15
  609.0 257.6 %all-reduce.12.cloned.1.call-start = ((), (), s32[]{:S(2)}) async-start(), calls=%async_computation.5 | async-start | bytes 262144 | tf_op jit(solution)/shard_map/psum | solution.py:15
  742.9 258.7 %all-reduce.14.cloned.1.call-start = ((), (), s32[]{:S(2)}) async-start(), calls=%async_computation.6 | async-start | bytes 262144 | tf_op jit(solution)/shard_map/psum | solution.py:15
  877.9 256.6 %all-reduce.16.cloned.1.call-start = ((), (), s32[]{:S(2)}) async-start(), calls=%async_computation.7 | async-start | bytes 262144 | tf_op jit(solution)/shard_map/psum | solution.py:15
  1010.8 258.7 %all-reduce.18.cloned.1.call-start = ((), (), s32[]{:S(2)}) async-start(), calls=%async_computation.8 | async-start | bytes 262144 | tf_op jit(solution)/shard_map/psum | solution.py:15
  1145.8 256.6 %all-reduce.20.cloned.1.call-start = ((), (), s32[]{:S(2)}) async-start(), calls=%async_computation.9 | async-start | bytes 262144 | tf_op jit(solution)/shard_map/psum | solution.py:15
  1278.7 258.7 %all-reduce.22.cloned.1.call-start = ((), (), s32[]{:S(2)}) async-start(), calls=%async_computation.10 | async-start | bytes 262144 | tf_op jit(solution)/shard_map/psum | solution.py:15
  1413.7 256.6 %all-reduce.24.cloned.1.call-start = ((), (), s32[]{:S(2)}) async-start(), calls=%async_computation.11 | async-start | bytes 262144 | tf_op jit(solution)/shard_map/psum | solution.py:15
Sparse Core Ops, SparseCore 0:
  417.6 181.6 reduce-scatter.1
  609.1 124.4 all-reduce.9
  743.0 123.5 all-reduce.11
  878.0 123.5 all-reduce.13
  1010.9 123.5 all-reduce.15
  1145.9 123.5 all-reduce.17
  1278.8 123.5 all-reduce.19
  1413.8 123.5 all-reduce.21
  1546.8 123.5 all-reduce.23
where the time goes:
time: 1690 us; the launch traced here: 1680 us
  waiting for transfers between devices  1450 us (86%)
  matrix products  95.6 us (6%)
  local copies, waits for them, and re-layouts  48.3 us (3%)
  other arithmetic  42.5 us (3%)
    psum x8, waiting for transfers between devices, converge_balancing(): totals = lax.psum(partial_totals, ('aa', 'ba'))  989 us
    reduce_scatter x1, waiting for transfers between devices, per_device(): lax.psum_scatter(jnp.einsum('qid,qjd->qij', left, right, preferred_elemen...  179 us
    all_to_all x1, waiting for transfers between devices, per_device(): lax.all_to_all(send_one, 'ba', split_axis=0, concat_axis=0, tiled=True)  146 us
    all_to_all x1, waiting for transfers between devices, per_device(): lax.all_to_all(second_seed_sender, 'ba', split_axis=0, concat_axis=0, til...  138 us
    dot_general x4, matrix products, per_device(): jnp.einsum('qij,qj->qi', exponential_affinity, jnp.take(col_scale, col_id...  34.8 us
  transfers between devices with their start and end apart: 11, of which 11 were waited for; matrix products, arithmetic and copies ran while one was open for 2% of the time, Pallas kernels for 0%

commit v1 on v0

v1 whole, which is shorter than its diff:
```python
import functools

import jax
import jax.numpy as jnp
from jax import lax
from jax.experimental import pallas as pl
from jax.experimental.pallas import tpu as pltpu
from jax.sharding import PartitionSpec as P

BS = 512
SWEEPS = 4
MESH = pl.DeviceIdType.MESH

smoothing_regularizer = 0.02
norm_floor = 1e-06


def exchange(buf, send_sem, recv_sem, step, axis, me, n):
    copies = []
    for d in range(1, n):
        peer = lax.rem(me + d, n)
        copy = pltpu.make_async_remote_copy(
            src_ref=buf.at[step, me],
            dst_ref=buf.at[step, me],
            send_sem=send_sem.at[step, d],
            recv_sem=recv_sem.at[step, me],
            device_id={axis: peer},
            device_id_type=MESH,
        )
        copy.start()
        copies.append(copy)
    for d in range(1, n):
        source = lax.rem(me + n - d, n)
        pltpu.make_async_remote_copy(
            src_ref=buf.at[step, source],
            dst_ref=buf.at[step, source],
            send_sem=send_sem.at[step, d],
            recv_sem=recv_sem.at[step, source],
            device_id={axis: source},
            device_id_type=MESH,
        ).wait_recv()
    for copy in copies:
        copy.wait_send()


def sweeps_kernel(
    n_aa,
    n_ba,
    row_src,
    col_src,
    cosine,
    same_one,
    same_two,
    final_one,
    final_two,
    row_out,
    col_out,
    k_hi,
    k_lo,
    kt_hi,
    kt_lo,
    part,
    full,
    part_send,
    part_recv,
    full_send,
    full_recv,
):
    a = lax.axis_index("aa")
    b = lax.axis_index("ba")
    owned = cosine.shape[0]
    barrier = pltpu.get_barrier_semaphore()
    for d in range(1, n_aa):
        pl.semaphore_signal(barrier, inc=1, device_id={"aa": lax.rem(a + d, n_aa)}, device_id_type=MESH)
    for d in range(1, n_ba):
        pl.semaphore_signal(barrier, inc=1, device_id={"ba": lax.rem(b + d, n_ba)}, device_id_type=MESH)

    def prepare(q, carry):
        k = jnp.exp(cosine[q] * (1.0 / smoothing_regularizer))
        hi = k.astype(jnp.bfloat16)
        k_hi[q] = hi
        k_lo[q] = (k - hi.astype(jnp.float32)).astype(jnp.bfloat16)
        kt = k.T
        hi = kt.astype(jnp.bfloat16)
        kt_hi[q] = hi
        kt_lo[q] = (kt - hi.astype(jnp.float32)).astype(jnp.bfloat16)
        return carry

    lax.fori_loop(0, owned, prepare, 0)
    pl.semaphore_wait(barrier, n_aa - 1 + n_ba - 1)

    ids = lax.broadcasted_iota(jnp.int32, (n_ba, BS), 0)
    lane_rows = lax.broadcasted_iota(jnp.int32, (16, BS), 0)

    def half(step, scale, source, target, hi_ref, lo_ref, same):
        def one(q, acc):
            v = jnp.sum(jnp.where(ids == source[q], scale, 0.0), axis=0, keepdims=True)
            v_hi = v.astype(jnp.bfloat16).astype(jnp.float32)
            v_lo = v - v_hi
            lhs = jnp.where(
                lane_rows == 0,
                jnp.broadcast_to(v_hi, (16, BS)),
                jnp.where(lane_rows == 1, jnp.broadcast_to(v_lo, (16, BS)), 0.0),
            ).astype(jnp.bfloat16)
            got = jnp.dot(lhs, hi_ref[q], preferred_element_type=jnp.float32) + jnp.dot(
                lhs, lo_ref[q], preferred_element_type=jnp.float32
            )
            term = jnp.sum(got, axis=0, keepdims=True)
            return acc + jnp.where(ids == target[q], jnp.broadcast_to(term, (n_ba, BS)), 0.0)

        part[step, a] = lax.fori_loop(0, owned, one, jnp.zeros((n_ba, BS), jnp.float32))
        exchange(part, part_send, part_recv, step, "aa", a, n_aa)
        mine = part[step, 0]
        for i in range(1, n_aa):
            mine = mine + part[step, i]
        full[step, b] = mine
        exchange(full, full_send, full_recv, step, "ba", b, n_ba)
        total = jnp.zeros((n_ba, BS), jnp.float32)
        for i in range(n_ba):
            total = total + jnp.where(same[i] > 0.0, full[step, i], 0.0)
        return 1.0 / (1.0 + total)

    def sweep(i, col_scale):
        row_scale = half(2 * i, col_scale, col_src, row_src, kt_hi, kt_lo, same_one)
        return half(2 * i + 1, row_scale, row_src, col_src, k_hi, k_lo, same_two)

    lax.fori_loop(0, SWEEPS, sweep, jnp.ones((n_ba, BS), jnp.float32))

    for step, final, out in ((2 * SWEEPS - 2, final_one, row_out), (2 * SWEEPS - 1, final_two, col_out)):
        total = jnp.zeros(out.shape, jnp.float32)
        for i in range(n_ba):
            row = full[step, i, pl.ds(b, 1), :]
            total = total + jnp.where(final[i] > 0.0, jnp.broadcast_to(row, out.shape), 0.0)
        out[...] = jnp.log(1.0 / (1.0 + total))


def balance(cosine, row_src, col_src, same_one, same_two, final_one, final_two, n_aa, n_ba, blocks_dev):
    owned = cosine.shape[0]
    vmem = pl.BlockSpec(memory_space=pltpu.VMEM)
    smem = pl.BlockSpec(memory_space=pltpu.SMEM)
    out = jax.ShapeDtypeStruct((blocks_dev, BS), jnp.float32)
    halves = pltpu.VMEM((owned, BS, BS), jnp.bfloat16)
    steps = 2 * SWEEPS
    return pl.pallas_call(
        functools.partial(sweeps_kernel, n_aa, n_ba),
        out_shape=(out, out),
        in_specs=[smem, smem] + [vmem] * 5,
        out_specs=(vmem, vmem),
        scratch_shapes=[
            halves,
            halves,
            halves,
            halves,
            pltpu.VMEM((steps, n_aa, n_ba, BS), jnp.float32),
            pltpu.VMEM((steps, n_ba, n_ba, BS), jnp.float32),
            pltpu.SemaphoreType.DMA((steps, n_aa)),
            pltpu.SemaphoreType.DMA((steps, n_aa)),
            pltpu.SemaphoreType.DMA((steps, n_ba)),
            pltpu.SemaphoreType.DMA((steps, n_ba)),
        ],
        compiler_params=pltpu.CompilerParams(collective_id=0, has_side_effects=True),
        name="sweeps",
    )(row_src, col_src, cosine, same_one, same_two, final_one, final_two)


def per_device(initial_dictionary_matrix, decoder_two, route_one, route_two, candidate_pair_slots):
    column = lax.axis_index("ba")
    depth = lax.axis_size("aa")
    depth_index = lax.axis_index("aa")
    owners = lax.axis_size("ba")
    width = initial_dictionary_matrix.shape[1]
    blocks_dev = initial_dictionary_matrix.shape[0] // BS
    sum_one = jnp.sum(jnp.square(initial_dictionary_matrix.astype(jnp.float32)), axis=1)
    sum_two = jnp.sum(jnp.square(decoder_two.astype(jnp.float32)), axis=1)
    sum_one, sum_two = lax.psum((sum_one, sum_two), "aa")
    unit_one = (
        initial_dictionary_matrix.astype(jnp.float32) * lax.rsqrt(sum_one + norm_floor)[:, None]
    ).astype(jnp.bfloat16)
    unit_two = (decoder_two.astype(jnp.float32) * lax.rsqrt(sum_two + norm_floor)[:, None]).astype(
        jnp.bfloat16
    )
    send_one = jnp.take(unit_one.reshape(blocks_dev, BS, width), route_one[column], axis=0)
    send_two = jnp.take(unit_two.reshape(blocks_dev, BS, width), route_two[column], axis=0)
    got_one, got_two = (
        lax.all_to_all(send_one, "ba", split_axis=0, concat_axis=0, tiled=True),
        lax.all_to_all(send_two, "ba", split_axis=0, concat_axis=0, tiled=True),
    )
    column_pairs = candidate_pair_slots[0]
    whole_pairs = column_pairs.shape[0]
    owned = whole_pairs // depth
    left = jnp.take(got_one, column_pairs[:, 0], axis=0)
    right = jnp.take(got_two, column_pairs[:, 1], axis=0)
    cosine = lax.psum_scatter(
        jnp.einsum("qid,qjd->qij", left, right, preferred_element_type=jnp.float32),
        "aa",
        scatter_dimension=0,
        tiled=True,
    )
    my_pairs = lax.dynamic_slice_in_dim(column_pairs, depth_index * owned, owned, 0)

    def masks(route):
        same = (route == route[:, column][:, None]).T
        final = route[column][:, None] == jnp.arange(blocks_dev, dtype=jnp.int32)[None, :]
        return (
            jnp.broadcast_to(same.astype(jnp.float32)[:, :, None], (owners, owners, BS)),
            jnp.broadcast_to(final.astype(jnp.float32)[:, :, None], (owners, blocks_dev, BS)),
        )

    same_one, final_one = masks(route_one)
    same_two, final_two = masks(route_two)
    row_log, col_log = balance(
        cosine,
        my_pairs[:, 0],
        my_pairs[:, 1],
        same_one,
        same_two,
        final_one,
        final_two,
        depth,
        owners,
        blocks_dev,
    )
    return (row_log.reshape(-1), col_log.reshape(-1))


def solution(mesh):
    placed = (P("ba", "aa"), P("ba", "aa"), P(), P(), P("ba", None, None))
    return jax.shard_map(
        per_device, mesh=mesh, in_specs=placed, out_specs=(P("ba"), P("ba")), check_vma=False
    )
```

time: 1690 us -> 698 us (0.41)
  waiting for transfers between devices: 1450 us -> 465 us
  Pallas kernels: 0 us -> 84.4 us
  matrix products: 95.6 us -> 26.2 us
    psum x8 -> x0, waiting for transfers between devices: 989 us -> none  [converge_balancing(): totals = lax.psum(partial_totals, ('aa', 'ba'))]
    pallas_call x0 -> x1, Pallas kernels: none -> 84.4 us  [balance(): pl.pallas_call(functools.partial(sweeps_kernel, n_aa, n_ba), out_shape=(o...]
    dot_general x16 -> x0, matrix products: 69.4 us -> none  [the longest x4 34.8 us: per_device(): jnp.einsum('qij,qj->qi', exponential_affinity, jnp.take(col_scale, col_id...]
  transfers between devices with their start and end apart: 11 -> 3, of which waited for: 11 -> 3; matrix products, arithmetic and copies ran while one was open for 2% -> 5% of each run, Pallas kernels for 0% -> 0%
where the time goes in v1:
time: 698 us; the launch traced here: 697 us
  waiting for transfers between devices  465 us (67%)
  Pallas kernels  84.4 us (12%)
  local copies, waits for them, and re-layouts  47.6 us (7%)
  other arithmetic  36.7 us (5%)
  matrix products  26.2 us (4%)
  between operations  14.1 us (2%)
  blocking collectives  12.9 us (2%)
  starting transfers between devices  10.9 us (2%)
    reduce_scatter x1, waiting for transfers between devices, per_device(): lax.psum_scatter(jnp.einsum('qid,qjd->qij', left, right, preferred_elemen...  180 us
    all_to_all x1, waiting for transfers between devices, per_device(): lax.all_to_all(send_two, 'ba', split_axis=0, concat_axis=0, tiled=True)  147 us
    all_to_all x1, waiting for transfers between devices, per_device(): lax.all_to_all(send_one, 'ba', split_axis=0, concat_axis=0, tiled=True)  138 us
    pallas_call x1, Pallas kernels, balance(): pl.pallas_call(functools.partial(sweeps_kernel, n_aa, n_ba), out_shape=(o...  84.4 us
    dot_general x1, matrix products, per_device(): jnp.einsum('qid,qjd->qij', left, right, preferred_element_type=jnp.float32)  26.2 us
  transfers between devices with their start and end apart: 3, of which 3 were waited for; matrix products, arithmetic and copies ran while one was open for 5% of the time, Pallas kernels for 0%

profile of v1, /device:TPU:0, one launch (start us, length us, event | category | flops | bytes accessed | tf_op | source)
XLA Modules:
  0.0 697.4 jit_solution(2701184697706266655)
XLA Ops:
  7.2 0.9 compare_and_fusion.3
  8.0 0.8 compare_and_fusion.1
  8.9 4.9 fusion.5
  13.8 1.5 fusion.7
  15.3 12.9 %all-reduce = (f32[4096]{0:T(1024)S(1)}, f32[4096]{0:T(1024)S(1)}) all-reduce(f32[4096]{0:T(1024)S(1)} %fusion.7, f32[4096]{0:T(1024)S(1)} %fusion.5), channel_id=1, replica_groups=mesh['aa'=4,'ba'=8] {'aa'}, use_global_device_ids=true, to_apply=%region_3.6 | all-reduce | flops 8192 | bytes 65536 | tf_op jit(solution)/shard_map/psum | solution.py:175
  28.2 7.3 %fusion.6 = bf16[4096,896]{1,0:T(8,128)(2,1)} fusion(bf16[4096,896]{1,0:T(8,128)(2,1)} %param.9, f32[4096]{0:T(1024)S(1)} %get-tuple-element.25), kind=kLoop, calls=%fused_computation.14 | loop fusion | flops 11010048 | bytes 14696448 | tf_op jit(solution)/shard_map/convert_element_type | solution.py:178
  35.5 7.4 %gather_fusion = bf16[8,512,896]{2,1,0:T(8,128)(2,1)} fusion(bf16[8,512,896]{2,1,0:T(8,128)(2,1)} %bitcast.29, s32[1024]{0:T(1024)S(1)} %pad_clamp_fusion.3), kind=kCustom, calls=%fused_computation.clone | custom fusion | bytes 14680096 | tf_op jit(solution)/shard_map/jit(_take)/gather | solution.py:182
  43.0 6.8 broadcast_select_fusion.1
  49.8 5.8 all-to-all-start
  55.7 7.4 %fusion.8 = bf16[4096,896]{1,0:T(8,128)(2,1)} fusion(bf16[4096,896]{1,0:T(8,128)(2,1)} %param.10, f32[4096]{0:T(1024)S(1)} %get-tuple-element.24), kind=kLoop, calls=%fused_computation.16 | loop fusion | flops 11010048 | bytes 14696448 | tf_op jit(solution)/shard_map/convert_element_type | solution.py:179
  63.0 7.4 %gather_fusion.2 = bf16[8,512,896]{2,1,0:T(8,128)(2,1)} fusion(bf16[8,512,896]{2,1,0:T(8,128)(2,1)} %bitcast.30, s32[1024]{0:T(1024)S(1)} %pad_clamp_fusion.1), kind=kCustom, calls=%fused_computation.2.clone | custom fusion | bytes 14680096 | tf_op jit(solution)/shard_map/jit(_take)/gather | solution.py:183
  70.4 6.8 broadcast_select_fusion
  77.2 138.1 %all-to-all-done = bf16[8,512,896]{2,1,0:T(8,128)(2,1)} async-done(((bf16[8,512,896]{2,1,0:T(8,128)(2,1)}), bf16[8,512,896]{2,1,0:T(8,128)(2,1)}, u32[]{:S(2)}, u32[]{:S(2)}) %all-to-all-start) | async-done | bytes 7340064 | tf_op jit(solution)/shard_map/all_to_all | solution.py:185
  215.4 4.8 all-to-all-start.1
  220.5 12.8 %gather_fusion.1 = bf16[24,512,896]{2,1,0:T(8,128)(2,1)} fusion(bf16[8,512,896]{2,1,0:T(8,128)(2,1)} %all-to-all-done, s32[1024]{0:T(1024)S(1)} %get-tuple-element.27), kind=kCustom, calls=%fused_computation.1.clone | custom fusion | bytes 44040288 | tf_op jit(solution)/shard_map/jit(_take)/gather | solution.py:191
  233.3 146.6 %all-to-all-done.1 = bf16[8,512,896]{2,1,0:T(8,128)(2,1)} async-done(((bf16[8,512,896]{2,1,0:T(8,128)(2,1)}), bf16[8,512,896]{2,1,0:T(8,128)(2,1)}, u32[]{:S(2)}, u32[]{:S(2)}) %all-to-all-start.1) | async-done | bytes 7340064 | tf_op jit(solution)/shard_map/all_to_all | solution.py:186
  379.9 12.6 %gather_fusion.3 = bf16[24,512,896]{2,1,0:T(8,128)(2,1)} fusion(bf16[8,512,896]{2,1,0:T(8,128)(2,1)} %all-to-all-done.1, s32[1024]{0:T(1024)S(1)} %get-tuple-element.26), kind=kCustom, calls=%fused_computation.3.clone | custom fusion | bytes 44040288 | tf_op jit(solution)/shard_map/jit(_take)/gather | solution.py:192
  392.5 26.2 %fusion = f32[24,512,512]{2,1,0:T(8,128)} fusion(bf16[24,512,896]{2,1,0:T(8,128)(2,1)} %gather_fusion.3, bf16[24,512,896]{2,1,0:T(8,128)(2,1)} %gather_fusion.1, pred[24]{0:T(512)(128)(4,1)S(1)} %get-tuple-element.18, pred[24]{0:T(512)(128)(4,1)S(1)} %get-tuple-element.10), kind=kOutput, calls=%fused_computation.4 | convolution fusion | flops 11296309248 | bytes 69206064 | tf_op jit(solution)/shard_map/qid,qjd->qij/dot_general | solution.py:194
  420.8 179.8 %reduce-scatter.2.cloned.1.call-done.cosine = f32[6,512,512]{2,1,0:T(8,128)} async-done(((f32[24,512,512]{2,1,0:T(8,128)}), f32[6,512,512]{2,1,0:T(8,128)}) %reduce-scatter.2.cloned.1.call-update) | async-done | bytes 6291472 | tf_op jit(solution)/shard_map/reduce_scatter | solution.py:193
  600.6 0.7 broadcast_in_dim.28.final_one
  601.3 0.7 broadcast_in_dim.29.final_two
  603.5 84.4 %sweeps.1 = (f32[8,512]{1,0:T(8,128)}, f32[8,512]{1,0:T(8,128)}) custom-call(s32[6]{0:T(128)} %get-tuple-element.21.row_src, s32[6]{0:T(128)} %get-tuple-element.20.col_src, f32[6,512,512]{2,1,0:T(8,128)} %reduce-scatter.2.cloned.1.call-done.cosine, f32[8,8,512]{2,1,0:T(8,128)} %broadcast_in_dim.26.same_one, f32[8,8,512]{2,1,0:T(8,128)} %broadcast_in_dim.27.same_two, ...), custom_call_target="tpu_custom_call" | custom-call | tf_op jit(solution)/shard_map/sweeps/pallas_call | solution.py:144
  687.9 1.3 copy.9
  689.2 1.3 copy.10
  (28 shorter events, 3.8 us)
Async XLA Ops:
  7.2 6.6 copy-start
  49.8 165.6 %all-to-all-start = ((bf16[8,512,896]{2,1,0:T(8,128)(2,1)}), bf16[8,512,896]{2,1,0:T(8,128)(2,1)}, u32[]{:S(2)}, u32[]{:S(2)}) async-start(bf16[8,512,896]{2,1,0:T(8,128)(2,1)} %broadcast_select_fusion.1), calls=%async_computation | async-start | bytes 14680064 | tf_op jit(solution)/shard_map/all_to_all | solution.py:185
  77.2 143.2 %copy-start.3 = (s32[1,24,2]{1,2,0:T(2,128)S(1)}, s32[1,24,2]{1,2,0:T(2,128)}, u32[]{:S(2)}) copy-start(s32[1,24,2]{1,2,0:T(2,128)} %param.13) | copy-start | bytes 580
  215.4 164.5 %all-to-all-start.1 = ((bf16[8,512,896]{2,1,0:T(8,128)(2,1)}), bf16[8,512,896]{2,1,0:T(8,128)(2,1)}, u32[]{:S(2)}, u32[]{:S(2)}) async-start(bf16[8,512,896]{2,1,0:T(8,128)(2,1)} %broadcast_select_fusion), calls=%async_computation.1 | async-start | bytes 14680064 | tf_op jit(solution)/shard_map/all_to_all | solution.py:186
  220.2 380.3 %reduce-scatter.2.cloned.1.call-start = ((), (), s32[]{:S(2)}) async-start(), calls=%async_computation.3 | async-start | bytes 31457280 | tf_op jit(solution)/shard_map/reduce_scatter | solution.py:193
  418.7 0.7 copy-start.1
  418.7 0.9 copy-start.2
Sparse Core Ops, SparseCore 0:
  418.8 181.6 reduce-scatter.1
